TPU v7x, 32 devices: a whole 2x2x4 slice. The times are simulated.
32 devices in a mesh: row: 8 (over z, x), col: 4 (over y, core).
Axes of the slice: x: 2, y: 2, z: 4, core: 2. Of those that a mesh axis runs over, the one named last changes fastest.
Arguments:
- inputs: bfloat16 [4, 2048, 768], P(None, ('row', 'col')), may hold values from -6 to 6
- cotangent: bfloat16 [4, 2048, 768], P(None, ('row', 'col')), may hold values from -16 to 16
- projector: bfloat16 [768, 2304], P('row', 'col'), may hold values from -0.21875 to 0.21875
- projector_bias: bfloat16 [2304], P('col'), may hold values from -2 to 2
- combiner: bfloat16 [768, 768], P('row', 'col'), may hold values from -6 to 6
- combiner_bias: float32 [768], replicated, may hold values from -2 to 2
- attend_gain: float32 [768], replicated, may hold values from 0.5 to 1.5
- attend_shift: float32 [768], replicated, may hold values from -2 to 2
- expander: bfloat16 [768, 3072], P('row', 'col'), may hold values from -0.21875 to 0.21875
- expander_bias: bfloat16 [3072], P('col'), may hold values from -2 to 2
- reducer: bfloat16 [3072, 768], P('col', 'row'), may hold values from -0.109375 to 0.109375
- reducer_bias: float32 [768], replicated, may hold values from -2 to 2
- final_gain: float32 [768], replicated, may hold values from 0.5 to 1.5
- final_shift: float32 [768], replicated, may hold values from -2 to 2
- projection: float32 [256, 64], replicated, may hold values from -4 to 4
- lengths: int32 [4], replicated, may hold values from 512 to 2048, as said below
Outputs:
- layer_output: bfloat16 [4, 2048, 768], P(None, ('row', 'col'))
- input_gradient: float32 [4, 2048, 768], P(None, ('row', 'col'))
- grad_projector: float32 [768, 2304], P('row', 'col')
- grad_projector_bias: float32 [2304], P('col')
- grad_combiner: float32 [768, 768], P('row', 'col')
- grad_combiner_bias: float32 [768], replicated
- grad_attend_gain: float32 [768], replicated
- grad_attend_shift: float32 [768], replicated
- grad_expander: float32 [768, 3072], P('row', 'col')
- grad_expander_bias: float32 [3072], P('col')
- grad_reducer: float32 [3072, 768], P('col', 'row')
- grad_reducer_bias: float32 [768], replicated
- grad_final_gain: float32 [768], replicated
- grad_final_shift: float32 [768], replicated
Inputs may be any that keep to these rules, and one draw needn't show every extreme that they name: `lengths`: slots at or past a sequence's length are padding. One sequence has 2048 valid slots and one has 512.
All inputs are finite; a program needn't handle non-finite values.
Results may differ from a plain program's by a relative error of at most 0.018.
Values may be sent and summed in bfloat16 or wider, within the bound.
No kernel may reach another device: no remote copies, remote signals or barrier semaphores. Data moves between devices by JAX's collectives and lax.ppermute only.
A program may use at most 192 MiB of HBM per device.

v0:
```python
import jax
import jax.numpy as jnp
from jax import lax
from jax.sharding import PartitionSpec as P

layer_eps = 1e-06
largest_logit = lax.Precision.HIGHEST


def layer_norm(values, gain_vector, shift_vector):
    midpoint_shift = values - jnp.mean(values, axis=-1, keepdims=True)
    spread = jnp.mean(midpoint_shift * midpoint_shift, axis=-1, keepdims=True)
    return midpoint_shift * lax.rsqrt(spread + layer_eps) * gain_vector + shift_vector


def feature_map(vectors, omegas):
    scaled = vectors * vectors.shape[-1] ** (-0.25)
    angles = jnp.einsum("thd,md->thm", scaled, omegas, precision=largest_logit)
    energy = 0.5 * jnp.sum(scaled * scaled, axis=-1, keepdims=True)
    return jnp.exp(angles - energy) * omegas.shape[0] ** (-0.5)


def key_summary(key_rows, value_matrix, keep_mask, omegas):
    key_random_features = feature_map(key_rows, omegas) * keep_mask[:, None, None]
    key_value_state = jnp.einsum(
        "oyu,oyb->yub", key_random_features, value_matrix, precision=largest_logit
    )
    return (key_value_state, jnp.sum(key_random_features, axis=0))


def query_read(query_rows, key_value_state, norm_total, omegas):
    query_random_features = feature_map(query_rows, omegas)
    numerator_rows = jnp.einsum(
        "uow,owe->uoe", query_random_features, key_value_state, precision=largest_logit
    )
    denom = jnp.einsum("thm,hm->th", query_random_features, norm_total, precision=largest_logit)
    return numerator_rows / denom[:, :, None]


def exact_gelu(values):
    return jax.nn.gelu(values, approximate=False)


def contract_rows(left_mat, right_mat):
    return lax.dot_general(
        left_mat, right_mat, (((0,), (0,)), ((), ())), preferred_element_type=jnp.float32
    )


def contract_cols(left_mat, right_mat):
    return lax.dot_general(
        left_mat, right_mat, (((1,), (1,)), ((), ())), preferred_element_type=jnp.float32
    )


def fetch_weights(projector, combiner, expander, reducer, projector_bias, expander_bias):
    project_cols, expand_cols, reduce_cols = (projector, expander, reducer)
    pbias_cols, ebias_cols = (projector_bias, expander_bias)
    gathered = (
        lax.all_gather(project_cols, "row", axis=0, tiled=True),
        lax.all_gather(combiner, "row", axis=0, tiled=True),
        lax.all_gather(expand_cols, "row", axis=0, tiled=True),
        lax.all_gather(reduce_cols, "row", axis=1, tiled=True),
    )
    combine_full = lax.all_gather(gathered[1], "col", axis=1, tiled=True)
    return (
        gathered[0],
        combine_full,
        gathered[2],
        gathered[3],
        pbias_cols.astype(jnp.float32),
        ebias_cols.astype(jnp.float32),
    )


def reduce_grads(project_sum, combine_sum, expand_sum, reduce_sum, pbias_sum, ebias_sum):
    combine_cols = lax.psum_scatter(
        combine_sum.astype(jnp.bfloat16), "col", scatter_dimension=1, tiled=True
    )
    row_total = lax.axis_size("row")
    reduced = (
        lax.psum_scatter(
            project_sum.astype(jnp.bfloat16), "row", scatter_dimension=0, tiled=True
        ).astype(jnp.float32),
        lax.psum_scatter(combine_cols, "row", scatter_dimension=0, tiled=True).astype(jnp.float32),
        lax.psum_scatter(
            expand_sum.astype(jnp.bfloat16), "row", scatter_dimension=0, tiled=True
        ).astype(jnp.float32),
        lax.psum_scatter(
            reduce_sum.astype(jnp.bfloat16), "row", scatter_dimension=1, tiled=True
        ).astype(jnp.float32),
        lax.psum_scatter(
            jnp.tile(pbias_sum, row_total).astype(jnp.bfloat16),
            "row",
            scatter_dimension=0,
            tiled=True,
        ).astype(jnp.float32),
        lax.psum_scatter(
            jnp.tile(ebias_sum, row_total).astype(jnp.bfloat16),
            "row",
            scatter_dimension=0,
            tiled=True,
        ).astype(jnp.float32),
    )
    return reduced


def on_device(
    inputs,
    cotangent,
    projector,
    projector_bias,
    combiner,
    combiner_bias,
    attend_gain,
    attend_shift,
    expander,
    expander_bias,
    reducer,
    reducer_bias,
    final_gain,
    final_shift,
    projection,
    lengths,
):
    row_total = lax.axis_size("row")
    col_total = lax.axis_size("col")
    micro_count = inputs.shape[0]
    token_count = inputs.shape[1]
    model_width = inputs.shape[2]
    head_size = projection.shape[1]
    head_count = model_width // head_size
    seq_slots = lengths.shape[0] // micro_count
    seq_length = token_count * row_total * col_total // seq_slots
    first_slot = (lax.axis_index("row") * col_total + lax.axis_index("col")) * token_count
    seq_place = first_slot // seq_length
    positions = first_slot % seq_length + jnp.arange(token_count, dtype=jnp.int32)
    slot_hot = (jnp.arange(seq_slots, dtype=jnp.int32) == seq_place).astype(jnp.float32)
    slot_four = slot_hot[:, None, None, None]
    slot_three = slot_hot[:, None, None]

    def micro_step(micro_index, weights):
        project_full, combine_full, expand_full, reduce_full, pbias_f, ebias_f = weights
        token_rows = inputs[micro_index]
        token_group = lax.all_gather(token_rows, "col", axis=0, tiled=True)
        mixed_local = (
            jnp.dot(token_group, project_full, preferred_element_type=jnp.float32) + pbias_f
        ).astype(jnp.bfloat16)
        mixed = lax.all_to_all(mixed_local, "col", split_axis=0, concat_axis=1, tiled=True)
        mixed_f = mixed.astype(jnp.float32)
        query_rows = mixed_f[:, :model_width].reshape(token_count, head_count, head_size)
        key_rows = mixed_f[:, model_width : 2 * model_width].reshape(
            token_count, head_count, head_size
        )
        value_matrix = mixed_f[:, 2 * model_width :].reshape(token_count, head_count, head_size)
        seq_bound = lengths[micro_index * seq_slots + seq_place]
        keep_mask = (positions < seq_bound).astype(jnp.float32)
        key_value_state, norm_total = key_summary(key_rows, value_matrix, keep_mask, projection)
        state_sums = lax.psum(
            (slot_four * key_value_state[None], slot_three * norm_total[None]), ("row", "col")
        )
        state_all = jnp.sum(slot_four * state_sums[0], axis=0)
        total_all = jnp.sum(slot_three * state_sums[1], axis=0)
        attended = (
            query_read(query_rows, state_all, total_all, projection)
            .reshape(token_count, model_width)
            .astype(jnp.bfloat16)
        )
        branch = jnp.dot(attended, combine_full, preferred_element_type=jnp.float32) + combiner_bias
        resid_attend = token_rows.astype(jnp.float32) + branch
        normed = layer_norm(resid_attend, attend_gain, attend_shift).astype(jnp.bfloat16)
        normed_group = lax.all_gather(normed, "col", axis=0, tiled=True)
        pre_act = jnp.dot(normed_group, expand_full, preferred_element_type=jnp.float32) + ebias_f
        hidden = exact_gelu(pre_act).astype(jnp.bfloat16)
        shrunk = (
            lax.psum_scatter(
                jnp.dot(hidden, reduce_full, preferred_element_type=jnp.float32).astype(
                    jnp.bfloat16
                ),
                "col",
                scatter_dimension=0,
                tiled=True,
            ).astype(jnp.float32)
            + reducer_bias
        )
        resid_final = normed.astype(jnp.float32) + shrunk
        layer_out, final_pull = jax.vjp(layer_norm, resid_final, final_gain, final_shift)
        grad_final, grad_fgain, grad_fshift = final_pull(cotangent[micro_index].astype(jnp.float32))
        shrink_grad = grad_final.astype(jnp.bfloat16)
        shrink_group = lax.all_gather(shrink_grad, "col", axis=0, tiled=True)
        hidden_grad = contract_cols(shrink_group, reduce_full)
        reduce_part = contract_rows(hidden, shrink_group)
        gelu_pull = jax.vjp(exact_gelu, pre_act)[1]
        pre_grad = gelu_pull(hidden_grad)[0].astype(jnp.bfloat16)
        expand_part = contract_rows(normed_group, pre_grad)
        ebias_part = jnp.sum(pre_grad.astype(jnp.float32), axis=0)
        normed_grad = grad_final + lax.psum_scatter(
            contract_cols(pre_grad, expand_full).astype(jnp.bfloat16),
            "col",
            scatter_dimension=0,
            tiled=True,
        ).astype(jnp.float32)
        attend_pull = jax.vjp(layer_norm, resid_attend, attend_gain, attend_shift)[1]
        resid_grad, grad_again, grad_ashift = attend_pull(normed_grad)
        branch_grad = resid_grad.astype(jnp.bfloat16)
        combine_part = contract_rows(attended, branch_grad)
        attended_grad = contract_cols(branch_grad, combine_full)
        read_pull = jax.vjp(
            lambda query_in, state_in, total_in: query_read(
                query_in, state_in, total_in, projection
            ),
            query_rows,
            state_all,
            total_all,
        )[1]
        query_grad, state_grad, total_grad = read_pull(
            attended_grad.reshape(token_count, head_count, head_size)
        )
        small_terms = jnp.stack(
            [
                grad_fgain,
                grad_fshift,
                grad_again,
                grad_ashift,
                jnp.sum(branch_grad.astype(jnp.float32), axis=0),
                jnp.sum(shrink_grad.astype(jnp.float32), axis=0),
            ]
        )
        summed = lax.psum(
            (slot_four * state_grad[None], slot_three * total_grad[None], small_terms),
            ("row", "col"),
        )
        state_back = jnp.sum(slot_four * summed[0], axis=0)
        total_back = jnp.sum(slot_three * summed[1], axis=0)
        summary_pull = jax.vjp(
            lambda key_in, value_in: key_summary(key_in, value_in, keep_mask, projection),
            key_rows,
            value_matrix,
        )[1]
        key_grad, value_grad = summary_pull((state_back, total_back))
        mixed_grad = jnp.concatenate(
            [
                query_grad.reshape(token_count, model_width),
                key_grad.reshape(token_count, model_width),
                value_grad.reshape(token_count, model_width),
            ],
            axis=1,
        ).astype(jnp.bfloat16)
        mixed_group = lax.all_to_all(mixed_grad, "col", split_axis=1, concat_axis=0, tiled=True)
        project_part = contract_rows(token_group, mixed_group)
        pbias_part = jnp.sum(mixed_group.astype(jnp.float32), axis=0)
        input_grad = resid_grad + lax.psum_scatter(
            contract_cols(mixed_group, project_full).astype(jnp.bfloat16),
            "col",
            scatter_dimension=0,
            tiled=True,
        ).astype(jnp.float32)
        parts = (project_part, combine_part, expand_part, reduce_part, pbias_part, ebias_part)
        return (layer_out.astype(jnp.bfloat16), input_grad, parts, summed[2])

    layer_outs = []
    input_grads = []
    small_acc = jnp.zeros((6, model_width), jnp.float32)
    shard_acc = (
        jnp.zeros(projector.shape, jnp.float32),
        jnp.zeros(combiner.shape, jnp.float32),
        jnp.zeros(expander.shape, jnp.float32),
        jnp.zeros(reducer.shape, jnp.float32),
        jnp.zeros(projector_bias.shape, jnp.float32),
        jnp.zeros(expander_bias.shape, jnp.float32),
    )
    for micro_index in range(micro_count):
        weights = fetch_weights(
            projector, combiner, expander, reducer, projector_bias, expander_bias
        )
        layer_out, input_grad, parts, small_sums = micro_step(micro_index, weights)
        layer_outs.append(layer_out)
        input_grads.append(input_grad)
        small_acc = small_acc + small_sums
        reduced = reduce_grads(*parts)
        shard_acc = tuple((running + update for running, update in zip(shard_acc, reduced)))
    return (
        jnp.stack(layer_outs),
        jnp.stack(input_grads),
        shard_acc[0],
        shard_acc[4],
        shard_acc[1],
        small_acc[4],
        small_acc[2],
        small_acc[3],
        shard_acc[2],
        shard_acc[5],
        shard_acc[3],
        small_acc[5],
        small_acc[0],
        small_acc[1],
    )


def solution(mesh):
    placed = (
        P(None, ("row", "col"), None),
        P(None, ("row", "col"), None),
        P("row", "col"),
        P("col"),
        P("row", "col"),
        P(),
        P(),
        P(),
        P("row", "col"),
        P("col"),
        P("col", "row"),
        P(),
        P(),
        P(),
        P(),
        P(),
    )
    return jax.shard_map(
        on_device,
        mesh=mesh,
        in_specs=placed,
        out_specs=(
            P(None, ("row", "col"), None),
            P(None, ("row", "col"), None),
            P("row", "col"),
            P("col"),
            P("row", "col"),
            P(),
            P(),
            P(),
            P("row", "col"),
            P("col"),
            P("col", "row"),
            P(),
            P(),
            P(),
        ),
        check_vma=False,
    )
```

profile of v0, /device:TPU:0, one launch (start us, length us, event | category | flops | bytes accessed | tf_op | source)
XLA Modules:
  0.0 1893.2 jit_solution(9473335730361034440)
XLA Ops:
  8.1 34.7 %all_gather.67 = bf16[768,576]{1,0:T(8,128)(2,1)S(1)} all-gather(bf16[96,576]{1,0:T(8,128)(2,1)} %param.18), channel_id=1, replica_groups=mesh['row'=8,'col'=4] {'row'}, dimensions={0}, use_global_device_ids=true | all-gather | bytes 995328 | tf_op jit(solution)/shard_map/all_gather | solution.py:60
  42.8 6.5 all-gather
  51.5 3.5 all-to-all-start
  54.9 9.7 all-gather.2
  66.8 6.6 all-gather.1
  73.4 3.5 all-to-all-start.2
  78.3 8.2 all-gather.3
  86.5 3.5 all-to-all-start.1
  92.1 4.6 all-to-all-done.1
  96.7 3.5 all-to-all-start.3
  123.7 31.8 %all_gather.68 = bf16[768,192]{1,0:T(8,128)(2,1)S(1)} all-gather(bf16[96,192]{1,0:T(8,128)(2,1)S(1)} %copy-done.168), channel_id=1, replica_groups=mesh['row'=8,'col'=4] {'row'}, dimensions={0}, use_global_device_ids=true | all-gather | bytes 331776 | tf_op jit(solution)/shard_map/all_gather | solution.py:61
  161.3 39.9 %all-reduce.9 = (f32[1,12,256]{2,1,0:T(8,128)S(1)}, f32[1,12,256]{2,1,0:T(8,128)S(1)}, f32[1,12,256]{2,1,0:T(8,128)S(1)}, f32[1,12,256]{2,1,0:T(8,128)S(1)}) all-reduce(f32[1,12,256]{2,1,0:T(8,128)S(1)} %multiply_bitcast_fusion.7, f32[1,12,256]{2,1,0:T(8,128)S(1)} %multiply_bitcast_fusion.5, ...), channel_id=1, replica_groups=mesh['row'=8,'col'=4] {'row','col'}, use_global_device_ids=true, to_apply=%region_4.5 | all-reduce | flops 12288 | bytes 98304 | tf_op jit(solution)/shard_map/psum | solution.py:159
  212.7 59.8 %all-reduce.22.cloned.1.call-done = (f32[1,12,256,64]{2,3,1,0:T(8,128)}, f32[1,12,256,64]{2,3,1,0:T(8,128)}, f32[1,12,256,64]{2,3,1,0:T(8,128)}, f32[1,12,256,64]{2,3,1,0:T(8,128)}) async-done(((f32[1,12,256,64]{2,3,1,0:T(8,128)}, f32[1,12,256,64]{2,3,1,0:T(8,128)}, f32[1,12,256,64]{2,3,1,0:T(8,128)}, f32[1,12,256,64]{2,3,1,0:T(8,128)}), (f32[1,12,256,64]{2,3,1,0:T(8,128)}, f32[1,12,256,64]{2,3,1,0:T(8,128)}, ...) | async-done | bytes 3145744 | tf_op jit(solution)/shard_map/psum | solution.py:159
  272.5 2.8 divide_convert_fusion
  287.6 6.8 all_gather.70
  294.4 7.0 all_gather.76
  301.4 7.2 all_gather.74
  308.6 7.0 all_gather.78
  315.7 4.7 multiply_convert_fusion.3
  320.3 2.7 convolution_convert_fusion.27
  323.1 4.6 multiply_convert_fusion.1
  329.8 4.6 multiply_convert_fusion.2
  336.5 4.7 multiply_convert_fusion
  344.6 21.3 %reduce-scatter.53.cloned.1.call-done = bf16[64,768]{1,0:T(8,128)(2,1)} async-done(((bf16[256,768]{1,0:T(8,128)(2,1)}), bf16[64,768]{1,0:T(8,128)(2,1)}) %reduce-scatter.53.cloned.1.call-update) | async-done | bytes 98320 | tf_op jit(solution)/shard_map/reduce_scatter | solution.py:176
  370.3 19.0 %reduce-scatter.51.cloned.1.call-done = bf16[64,768]{1,0:T(8,128)(2,1)} async-done(((bf16[256,768]{1,0:T(8,128)(2,1)}), bf16[64,768]{1,0:T(8,128)(2,1)}) %reduce-scatter.51.cloned.1.call-update) | async-done | bytes 98320 | tf_op jit(solution)/shard_map/reduce_scatter | solution.py:176
  389.3 23.3 %reduce-scatter.55.cloned.1.call-done = bf16[64,768]{1,0:T(8,128)(2,1)} async-done(((bf16[256,768]{1,0:T(8,128)(2,1)}), bf16[64,768]{1,0:T(8,128)(2,1)}) %reduce-scatter.55.cloned.1.call-update) | async-done | bytes 98320 | tf_op jit(solution)/shard_map/reduce_scatter | solution.py:176
  420.1 6.1 all_gather.81
  430.9 7.0 all_gather.80
  437.9 6.6 all_gather.82
  444.5 2.8 fusion.319
  449.4 3.2 fusion.317
  459.6 6.6 all_gather.79
  466.1 3.1 fusion.316
  476.2 21.3 %reduce-scatter.61.cloned.1.call-done = bf16[64,768]{1,0:T(8,128)(2,1)} async-done(((bf16[256,768]{1,0:T(8,128)(2,1)}), bf16[64,768]{1,0:T(8,128)(2,1)}) %reduce-scatter.61.cloned.1.call-update) | async-done | bytes 98320 | tf_op jit(solution)/shard_map/reduce_scatter | solution.py:197
  503.1 17.7 reduce-scatter.57.cloned.1.call-done
  550.8 2.7 convolution_convert_fusion.5
  556.2 2.6 convolution_convert_fusion.7
  577.7 2.7 convolution_convert_fusion.3
  591.5 79.0 %all-reduce.18.cloned.1.call-done = (f32[1,12,256]{2,1,0:T(8,128)}, f32[1,12,256]{2,1,0:T(8,128)}, f32[1,12,256]{2,1,0:T(8,128)}, f32[1,12,256]{2,1,0:T(8,128)}, f32[6,768]{1,0:T(8,128)}) async-done(((f32[1,12,256]{2,1,0:T(8,128)}, f32[1,12,256]{2,1,0:T(8,128)}, f32[1,12,256]{2,1,0:T(8,128)}, f32[1,12,256]{2,1,0:T(8,128)}, f32[6,768]{1,0:T(8,128)}), (f32[1,12,256]{2,1,0:T(8,128)}, f32[1,12,256]{2,1,0:T(8,128)}, ...) | async-done | bytes 67600 | tf_op jit(solution)/shard_map/psum | solution.py:229
  673.3 151.3 %all-reduce.20.cloned.1.call-done = (f32[1,12,256,64]{2,3,1,0:T(8,128)}, f32[1,12,256,64]{2,3,1,0:T(8,128)}, f32[1,12,256,64]{2,3,1,0:T(8,128)}, f32[1,12,256,64]{2,3,1,0:T(8,128)}) async-done(((f32[1,12,256,64]{2,3,1,0:T(8,128)}, f32[1,12,256,64]{2,3,1,0:T(8,128)}, f32[1,12,256,64]{2,3,1,0:T(8,128)}, f32[1,12,256,64]{2,3,1,0:T(8,128)}), (f32[1,12,256,64]{2,3,1,0:T(8,128)}, f32[1,12,256,64]{2,3,1,0:T(8,128)}, ...) | async-done | bytes 3145744 | tf_op jit(solution)/shard_map/psum | solution.py:229
  830.4 3.5 all-to-all-start.7
  845.3 3.5 all-to-all-start.6
  849.9 5.6 all-to-all-done.6
  855.5 3.7 all-to-all-start.5
  860.5 5.4 all-to-all-done.5
  865.9 3.5 all-to-all-start.4
  899.4 28.9 %reduce-scatter.81.cloned.1.call-done = bf16[96,768]{1,0:T(8,128)(2,1)} async-done(((bf16[768,768]{1,0:T(8,128)(2,1)}), bf16[96,768]{1,0:T(8,128)(2,1)}) %reduce-scatter.81.cloned.1.call-update) | async-done | bytes 147472 | tf_op jit(solution)/shard_map/reduce_scatter | solution.py:86
  932.1 63.3 %reduce-scatter.95.cloned.1.call-done = bf16[768,96]{0,1:T(8,128)(2,1)} async-done(((bf16[768,768]{0,1:T(8,128)(2,1)}), bf16[768,96]{0,1:T(8,128)(2,1)}) %reduce-scatter.95.cloned.1.call-update) | async-done | bytes 147472 | tf_op jit(solution)/shard_map/reduce_scatter | solution.py:89
  995.4 67.0 %reduce-scatter.93.cloned.1.call-done = bf16[768,96]{0,1:T(8,128)(2,1)} async-done(((bf16[768,768]{0,1:T(8,128)(2,1)}), bf16[768,96]{0,1:T(8,128)(2,1)}) %reduce-scatter.93.cloned.1.call-update) | async-done | bytes 147472 | tf_op jit(solution)/shard_map/reduce_scatter | solution.py:89
  1062.4 67.0 %reduce-scatter.91.cloned.1.call-done = bf16[768,96]{0,1:T(8,128)(2,1)} async-done(((bf16[768,768]{0,1:T(8,128)(2,1)}), bf16[768,96]{0,1:T(8,128)(2,1)}) %reduce-scatter.91.cloned.1.call-update) | async-done | bytes 147472 | tf_op jit(solution)/shard_map/reduce_scatter | solution.py:89
  1129.4 66.9 %reduce-scatter.89.cloned.1.call-done = bf16[768,96]{0,1:T(8,128)(2,1)} async-done(((bf16[768,768]{0,1:T(8,128)(2,1)}), bf16[768,96]{0,1:T(8,128)(2,1)}) %reduce-scatter.89.cloned.1.call-update) | async-done | bytes 147472 | tf_op jit(solution)/shard_map/reduce_scatter | solution.py:89
  1198.2 72.9 %all-reduce.24.cloned.1.call-done = (bf16[4608]{0:T(1024)(128)(2,1)}, bf16[4608]{0:T(1024)(128)(2,1)}, bf16[4608]{0:T(1024)(128)(2,1)}, bf16[4608]{0:T(1024)(128...) async-done(((bf16[4608]{0:T(1024)(128)(2,1)}, bf16[4608]{0:T(1024)(128)(2,1)}, ...) | async-done | bytes 86032
  1273.9 20.2 %reduce-scatter.71.cloned.1.call-done = bf16[64,768]{1,0:T(8,128)(2,1)} async-done(((bf16[256,768]{1,0:T(8,128)(2,1)}), bf16[64,768]{1,0:T(8,128)(2,1)}) %reduce-scatter.71.cloned.1.call-update) | async-done | bytes 98320 | tf_op jit(solution)/shard_map/reduce_scatter | solution.py:252
  1295.1 22.3 %reduce-scatter.67.cloned.1.call-done = bf16[64,768]{1,0:T(8,128)(2,1)} async-done(((bf16[256,768]{1,0:T(8,128)(2,1)}), bf16[64,768]{1,0:T(8,128)(2,1)}) %reduce-scatter.67.cloned.1.call-update) | async-done | bytes 98320 | tf_op jit(solution)/shard_map/reduce_scatter | solution.py:252
  1318.4 22.3 %reduce-scatter.63.cloned.1.call-done = bf16[64,768]{1,0:T(8,128)(2,1)} async-done(((bf16[256,768]{1,0:T(8,128)(2,1)}), bf16[64,768]{1,0:T(8,128)(2,1)}) %reduce-scatter.63.cloned.1.call-update) | async-done | bytes 98320 | tf_op jit(solution)/shard_map/reduce_scatter | solution.py:252
  1341.7 22.1 %reduce-scatter.59.cloned.1.call-done = bf16[64,768]{1,0:T(8,128)(2,1)} async-done(((bf16[256,768]{1,0:T(8,128)(2,1)}), bf16[64,768]{1,0:T(8,128)(2,1)}) %reduce-scatter.59.cloned.1.call-update) | async-done | bytes 98320 | tf_op jit(solution)/shard_map/reduce_scatter | solution.py:252
  1365.8 62.7 %reduce-scatter.111.cloned.1.call-done = bf16[96,192]{1,0:T(8,128)(2,1)} async-done(((bf16[768,192]{1,0:T(8,128)(2,1)}), bf16[96,192]{1,0:T(8,128)(2,1)}) %reduce-scatter.111.cloned.1.call-update) | async-done | bytes 36880
  1429.4 62.9 %reduce-scatter.109.cloned.1.call-done = bf16[96,192]{1,0:T(8,128)(2,1)} async-done(((bf16[768,192]{1,0:T(8,128)(2,1)}), bf16[96,192]{1,0:T(8,128)(2,1)}) %reduce-scatter.109.cloned.1.call-update) | async-done | bytes 36880
  1493.2 62.7 %reduce-scatter.107.cloned.1.call-done = bf16[96,192]{1,0:T(8,128)(2,1)} async-done(((bf16[768,192]{1,0:T(8,128)(2,1)}), bf16[96,192]{1,0:T(8,128)(2,1)}) %reduce-scatter.107.cloned.1.call-update) | async-done | bytes 36880
  1556.9 62.7 %reduce-scatter.105.cloned.1.call-done = bf16[96,192]{1,0:T(8,128)(2,1)} async-done(((bf16[768,192]{1,0:T(8,128)(2,1)}), bf16[96,192]{1,0:T(8,128)(2,1)}) %reduce-scatter.105.cloned.1.call-update) | async-done | bytes 36880
  1621.3 64.1 %reduce-scatter.103.cloned.1.call-done = bf16[96,576]{1,0:T(8,128)(2,1)} async-done(((bf16[768,576]{1,0:T(8,128)(2,1)}), bf16[96,576]{1,0:T(8,128)(2,1)}) %reduce-scatter.103.cloned.1.call-update) | async-done | bytes 110608
  1686.4 65.1 %reduce-scatter.101.cloned.1.call-done = bf16[96,576]{1,0:T(8,128)(2,1)} async-done(((bf16[768,576]{1,0:T(8,128)(2,1)}), bf16[96,576]{1,0:T(8,128)(2,1)}) %reduce-scatter.101.cloned.1.call-update) | async-done | bytes 110608
  1752.6 64.7 %reduce-scatter.99.cloned.1.call-done = bf16[96,576]{1,0:T(8,128)(2,1)} async-done(((bf16[768,576]{1,0:T(8,128)(2,1)}), bf16[96,576]{1,0:T(8,128)(2,1)}) %reduce-scatter.99.cloned.1.call-update) | async-done | bytes 110608
  1818.2 65.2 %reduce-scatter.97.cloned.1.call-done = bf16[96,576]{1,0:T(8,128)(2,1)} async-done(((bf16[768,576]{1,0:T(8,128)(2,1)}), bf16[96,576]{1,0:T(8,128)(2,1)}) %reduce-scatter.97.cloned.1.call-update) | async-done | bytes 110608
  (1014 shorter events, 239.3 us)
Async XLA Ops:
  8.0 105.3 %copy-start = (f32[256,64]{0,1:T(8,128)S(1)}, f32[256,64]{0,1:T(8,128)}, u32[]{:S(2)}) copy-start(f32[256,64]{0,1:T(8,128)} %param.30) | copy-start | bytes 196612
  51.5 21.9 %all-to-all-start = ((bf16[4,64,576]{2,1,0:T(8,128)(2,1)}), bf16[4,64,576]{2,1,0:T(8,128)(2,1)S(1)}, u32[]{:S(2)}, u32[]{:S(2)}) async-start(bf16[4,64,576]{2,1,0:T(8,128)(2,1)} %bitcast.2), calls=%async_computation | async-start | bytes 655360 | tf_op jit(solution)/shard_map/all_to_all | solution.py:149
  73.4 13.1 all-to-all-start.2
  86.5 10.2 all-to-all-start.1
  96.7 10.2 all-to-all-start.3
  100.1 172.3 %all-reduce.22.cloned.1.call-start = ((), (), s32[]{:S(2)}) async-start(), calls=%async_computation.77 | async-start | bytes 6291456 | tf_op jit(solution)/shard_map/psum | solution.py:159
  122.9 152.3 %all-gather.8.cloned.1.call-start = ((), (), s32[]{:S(2)}) async-start(), calls=%async_computation.40 | async-start | bytes 1474560 | tf_op jit(solution)/shard_map/all_gather | solution.py:65
  156.4 159.3 %all-gather.10.cloned.1.call-start = ((), (), s32[]{:S(2)}) async-start(), calls=%async_computation.41 | async-start | bytes 1327104 | tf_op jit(solution)/shard_map/all_gather | solution.py:62
  156.9 163.4 %all-gather.12.cloned.1.call-start = ((), (), s32[]{:S(2)}) async-start(), calls=%async_computation.42 | async-start | bytes 1327104 | tf_op jit(solution)/shard_map/all_gather | solution.py:63
  157.5 186.0 %reduce-scatter.49.cloned.1.call-start = ((), (), s32[]{:S(2)}) async-start(), calls=%async_computation.43 | async-start | bytes 491520 | tf_op jit(solution)/shard_map/reduce_scatter | solution.py:176
  283.0 191.1 %copy-start.37 = (f32[64,768]{1,0:T(8,128)}, f32[64,768]{1,0:T(8,128)S(1)}, u32[]{:S(2)}) copy-start(f32[64,768]{1,0:T(8,128)S(1)} %get-tuple-element.277) | copy-start | bytes 589828
  323.0 42.9 %reduce-scatter.53.cloned.1.call-start = ((), (), s32[]{:S(2)}) async-start(), calls=%async_computation.45 | async-start | bytes 491520 | tf_op jit(solution)/shard_map/reduce_scatter | solution.py:176
  329.7 59.6 %reduce-scatter.51.cloned.1.call-start = ((), (), s32[]{:S(2)}) async-start(), calls=%async_computation.44 | async-start | bytes 491520 | tf_op jit(solution)/shard_map/reduce_scatter | solution.py:176
  336.4 76.2 %reduce-scatter.55.cloned.1.call-start = ((), (), s32[]{:S(2)}) async-start(), calls=%async_computation.46 | async-start | bytes 491520 | tf_op jit(solution)/shard_map/reduce_scatter | solution.py:176
  341.9 70.7 %copy-start.43 = (bf16[64,768]{1,0:T(8,128)(2,1)S(1)}, bf16[64,768]{1,0:T(8,128)(2,1)}, u32[]{:S(2)}) copy-start(bf16[64,768]{1,0:T(8,128)(2,1)} %copy-done.42) | copy-start | bytes 294916
  341.9 70.7 %copy-start.163 = (f32[768]{0:T(1024)S(1)}, f32[768]{0:T(1024)}, u32[]{:S(2)}) copy-start(f32[768]{0:T(1024)} %param.28) | copy-start | bytes 9220
  343.2 128.6 %reduce-scatter.65.cloned.1.call-start = ((), (), s32[]{:S(2)}) async-start(), calls=%async_computation.51 | async-start | bytes 491520 | tf_op jit(solution)/shard_map/reduce_scatter | solution.py:197
  418.9 78.6 %copy-start.225 = (f32[64]{0:T(128)}, f32[64]{0:T(128)S(1)}, u32[]{:S(2)}) copy-start(f32[64]{0:T(128)S(1)} %negate_multiply_fusion.17) | copy-start | bytes 772
  429.6 44.5 %reduce-scatter.69.cloned.1.call-start = ((), (), s32[]{:S(2)}) async-start(), calls=%async_computation.53 | async-start | bytes 491520 | tf_op jit(solution)/shard_map/reduce_scatter | solution.py:197
  449.3 48.2 %reduce-scatter.61.cloned.1.call-start = ((), (), s32[]{:S(2)}) async-start(), calls=%async_computation.49 | async-start | bytes 491520 | tf_op jit(solution)/shard_map/reduce_scatter | solution.py:197
  454.7 66.1 %reduce-scatter.57.cloned.1.call-start = ((), (), s32[]{:S(2)}) async-start(), calls=%async_computation.47 | async-start | bytes 491520 | tf_op jit(solution)/shard_map/reduce_scatter | solution.py:197
  471.3 199.2 %all-reduce.18.cloned.1.call-start = ((), (), s32[]{:S(2)}) async-start(), calls=%async_computation.75 | async-start | bytes 180224 | tf_op jit(solution)/shard_map/psum | solution.py:229
  538.7 286.0 %all-reduce.20.cloned.1.call-start = ((), (), s32[]{:S(2)}) async-start(), calls=%async_computation.76 | async-start | bytes 6291456 | tf_op jit(solution)/shard_map/psum | solution.py:229
  540.6 341.8 %reduce-scatter.79.cloned.1.call-start = ((), (), s32[]{:S(2)}) async-start(), calls=%async_computation.58 | async-start | bytes 1474560 | tf_op jit(solution)/shard_map/reduce_scatter | solution.py:77
  543.0 341.3 %reduce-scatter.77.cloned.1.call-start = ((), (), s32[]{:S(2)}) async-start(), calls=%async_computation.57 | async-start | bytes 1474560 | tf_op jit(solution)/shard_map/reduce_scatter | solution.py:77
  544.7 341.7 %reduce-scatter.75.cloned.1.call-start = ((), (), s32[]{:S(2)}) async-start(), calls=%async_computation.56 | async-start | bytes 1474560 | tf_op jit(solution)/shard_map/reduce_scatter | solution.py:77
  546.4 342.1 %reduce-scatter.73.cloned.1.call-start = ((), (), s32[]{:S(2)}) async-start(), calls=%async_computation.55 | async-start | bytes 1474560 | tf_op jit(solution)/shard_map/reduce_scatter | solution.py:77
  548.0 351.4 %reduce-scatter.87.cloned.1.call-start = ((), (), s32[]{:S(2)}) async-start(), calls=%async_computation.62 | async-start | bytes 1327104 | tf_op jit(solution)/shard_map/reduce_scatter | solution.py:86
  550.7 348.7 %reduce-scatter.85.cloned.1.call-start = ((), (), s32[]{:S(2)}) async-start(), calls=%async_computation.61 | async-start | bytes 1327104 | tf_op jit(solution)/shard_map/reduce_scatter | solution.py:86
  553.4 346.0 %reduce-scatter.83.cloned.1.call-start = ((), (), s32[]{:S(2)}) async-start(), calls=%async_computation.60 | async-start | bytes 1327104 | tf_op jit(solution)/shard_map/reduce_scatter | solution.py:86
  556.1 372.2 %reduce-scatter.81.cloned.1.call-start = ((), (), s32[]{:S(2)}) async-start(), calls=%async_computation.59 | async-start | bytes 1327104 | tf_op jit(solution)/shard_map/reduce_scatter | solution.py:86
  558.9 436.6 %reduce-scatter.95.cloned.1.call-start = ((), (), s32[]{:S(2)}) async-start(), calls=%async_computation.66 | async-start | bytes 1327104 | tf_op jit(solution)/shard_map/reduce_scatter | solution.py:89
  561.5 500.9 %reduce-scatter.93.cloned.1.call-start = ((), (), s32[]{:S(2)}) async-start(), calls=%async_computation.65 | async-start | bytes 1327104 | tf_op jit(solution)/shard_map/reduce_scatter | solution.py:89
  564.2 565.1 %reduce-scatter.91.cloned.1.call-start = ((), (), s32[]{:S(2)}) async-start(), calls=%async_computation.64 | async-start | bytes 1327104 | tf_op jit(solution)/shard_map/reduce_scatter | solution.py:89
  566.9 629.5 %reduce-scatter.89.cloned.1.call-start = ((), (), s32[]{:S(2)}) async-start(), calls=%async_computation.63 | async-start | bytes 1327104 | tf_op jit(solution)/shard_map/reduce_scatter | solution.py:89
  589.7 235.0 %copy-start.28 = (f32[64,12,256]{2,0,1:T(8,128)S(1)}, f32[64,12,256]{2,0,1:T(8,128)}, u32[]{:S(2)}) copy-start(f32[64,12,256]{2,0,1:T(8,128)} %copy-done.27) | copy-start | bytes 2359300
  589.7 235.0 %copy-start.214 = (f32[64]{0:T(128)S(1)}, f32[64]{0:T(128)}, u32[]{:S(2)}) copy-start(f32[64]{0:T(128)} %copy-done.213) | copy-start | bytes 772
  591.5 235.5 %copy-start.71 = (bf16[64,768]{0,1:T(8,128)(2,1)S(1)}, bf16[64,768]{0,1:T(8,128)(2,1)}, u32[]{:S(2)}) copy-start(bf16[64,768]{0,1:T(8,128)(2,1)} %copy-done.70) | copy-start | bytes 294916
  591.5 235.5 %copy-start.246 = (f32[64]{0:T(128)S(1)}, f32[64]{0:T(128)}, u32[]{:S(2)}) copy-start(f32[64]{0:T(128)} %get-tuple-element.302) | copy-start | bytes 772
  830.4 14.9 all-to-all-start.7
  845.3 10.2 all-to-all-start.6
  855.5 10.4 all-to-all-start.5
  865.9 10.2 all-to-all-start.4
  869.4 401.8 %all-reduce.24.cloned.1.call-start = ((), (), s32[]{:S(2)}) async-start(), calls=%async_computation.78 | async-start | bytes 180224
  876.9 417.3 %reduce-scatter.71.cloned.1.call-start = ((), (), s32[]{:S(2)}) async-start(), calls=%async_computation.54 | async-start | bytes 491520 | tf_op jit(solution)/shard_map/reduce_scatter | solution.py:252
  878.2 439.2 %reduce-scatter.67.cloned.1.call-start = ((), (), s32[]{:S(2)}) async-start(), calls=%async_computation.52 | async-start | bytes 491520 | tf_op jit(solution)/shard_map/reduce_scatter | solution.py:252
  879.6 461.1 %reduce-scatter.63.cloned.1.call-start = ((), (), s32[]{:S(2)}) async-start(), calls=%async_computation.50 | async-start | bytes 491520 | tf_op jit(solution)/shard_map/reduce_scatter | solution.py:252
  880.9 482.9 %reduce-scatter.59.cloned.1.call-start = ((), (), s32[]{:S(2)}) async-start(), calls=%async_computation.48 | async-start | bytes 491520 | tf_op jit(solution)/shard_map/reduce_scatter | solution.py:252
  882.3 546.2 %reduce-scatter.111.cloned.1.call-start = ((), (), s32[]{:S(2)}) async-start(), calls=%async_computation.74 | async-start | bytes 442368
  884.3 608.0 %reduce-scatter.109.cloned.1.call-start = ((), (), s32[]{:S(2)}) async-start(), calls=%async_computation.73 | async-start | bytes 442368
  886.3 669.6 %reduce-scatter.107.cloned.1.call-start = ((), (), s32[]{:S(2)}) async-start(), calls=%async_computation.72 | async-start | bytes 442368
  888.3 731.2 %reduce-scatter.105.cloned.1.call-start = ((), (), s32[]{:S(2)}) async-start(), calls=%async_computation.71 | async-start | bytes 442368
  890.3 795.1 %reduce-scatter.103.cloned.1.call-start = ((), (), s32[]{:S(2)}) async-start(), calls=%async_computation.70 | async-start | bytes 1105920
  892.2 859.3 %reduce-scatter.101.cloned.1.call-start = ((), (), s32[]{:S(2)}) async-start(), calls=%async_computation.69 | async-start | bytes 1105920
  894.0 923.2 %reduce-scatter.99.cloned.1.call-start = ((), (), s32[]{:S(2)}) async-start(), calls=%async_computation.68 | async-start | bytes 1105920
  896.0 987.5 %reduce-scatter.97.cloned.1.call-start = ((), (), s32[]{:S(2)}) async-start(), calls=%async_computation.67 | async-start | bytes 1105920
  932.0 362.1 %copy-start.85 = (f32[64,768]{1,0:T(8,128)S(1)}, f32[64,768]{1,0:T(8,128)}, u32[]{:S(2)}) copy-start(f32[64,768]{1,0:T(8,128)} %copy-done.84) | copy-start | bytes 589828
  932.0 362.1 %copy-start.236 = (f32[64]{0:T(128)S(1)}, f32[64]{0:T(128)}, u32[]{:S(2)}) copy-start(f32[64]{0:T(128)} %copy-done.235) | copy-start | bytes 772
  932.0 385.4 %copy-start.87 = (f32[64,768]{1,0:T(8,128)S(1)}, f32[64,768]{1,0:T(8,128)}, u32[]{:S(2)}) copy-start(f32[64,768]{1,0:T(8,128)} %copy-done.86) | copy-start | bytes 589828
  932.0 385.4 %copy-start.238 = (f32[64]{0:T(128)S(1)}, f32[64]{0:T(128)}, u32[]{:S(2)}) copy-start(f32[64]{0:T(128)} %copy-done.237) | copy-start | bytes 772
  932.1 408.7 %copy-start.75 = (f32[64,768]{1,0:T(8,128)S(1)}, f32[64,768]{1,0:T(8,128)}, u32[]{:S(2)}) copy-start(f32[64,768]{1,0:T(8,128)} %copy-done.74) | copy-start | bytes 589828
  932.1 408.7 %copy-start.242 = (f32[64]{0:T(128)S(1)}, f32[64]{0:T(128)}, u32[]{:S(2)}) copy-start(f32[64]{0:T(128)} %copy-done.241) | copy-start | bytes 772
  932.1 431.8 %copy-start.73 = (f32[64,768]{1,0:T(8,128)S(1)}, f32[64,768]{1,0:T(8,128)}, u32[]{:S(2)}) copy-start(f32[64,768]{1,0:T(8,128)} %copy-done.72) | copy-start | bytes 589828
  932.1 431.8 %copy-start.240 = (f32[64]{0:T(128)S(1)}, f32[64]{0:T(128)}, u32[]{:S(2)}) copy-start(f32[64]{0:T(128)} %copy-done.239) | copy-start | bytes 772
  (258 other events, 1464.7 us)
Sparse Core Ops, SparseCore 0:
  123.0 149.3 all-reduce.21
  538.8 131.5 all-reduce.17
  678.0 146.5 all-reduce.19
Sparse Core Ops, SparseCore 1:
  156.4 17.6 all-gather.7
  176.2 41.4 all-gather.9
  219.8 42.9 all-gather.11
  323.1 19.3 reduce-scatter.48
  345.1 20.7 reduce-scatter.52
  368.6 20.7 reduce-scatter.50
  391.9 20.7 reduce-scatter.54
  429.6 21.1 reduce-scatter.64
  453.3 20.7 reduce-scatter.68
  476.7 20.7 reduce-scatter.60
  500.0 20.7 reduce-scatter.56
  544.1 25.7 reduce-scatter.78
  572.3 25.7 reduce-scatter.76
  600.8 25.6 reduce-scatter.74
  629.1 25.9 reduce-scatter.72
  658.9 65.8 reduce-scatter.86
  728.5 63.5 reduce-scatter.84
  795.9 65.4 reduce-scatter.82
  865.0 63.2 reduce-scatter.80
  932.1 63.2 reduce-scatter.94
  999.1 63.3 reduce-scatter.92
  1066.0 63.3 reduce-scatter.90
  1133.0 63.2 reduce-scatter.88
  1201.2 69.9 all-reduce.23
  1274.1 20.0 reduce-scatter.70
  1296.7 20.7 reduce-scatter.66
  1320.0 20.7 reduce-scatter.62
  1343.1 20.7 reduce-scatter.58
  1367.0 61.4 reduce-scatter.110
  1431.8 60.5 reduce-scatter.108
  1495.5 60.4 reduce-scatter.106
  1559.1 60.4 reduce-scatter.104
  1623.0 62.4 reduce-scatter.102
  1689.0 62.5 reduce-scatter.100
  1754.7 62.4 reduce-scatter.98
  1820.9 62.4 reduce-scatter.96
where the time goes:
time: 1900 us; the launch traced here: 1890 us
  waiting for transfers between devices  1380 us (73%)
  blocking collectives  192 us (10%)
  matrix products  133 us (7%)
  local copies, waits for them, and re-layouts  79.4 us (4%)
  other arithmetic  58.1 us (3%)
  starting transfers between devices  30.6 us (2%)
  between operations  21.7 us (1%)
    unnamed x48, waiting for transfers between devices  585 us
    reduce_scatter x4, waiting for transfers between devices, reduce_grads(): lax.psum_scatter(reduce_sum.astype(jnp.bfloat16), 'row', scatter_dimensio...  264 us
    psum x2, waiting for transfers between devices, micro_step(): lax.psum((slot_four * state_grad[None], slot_three * total_grad[None], sm...  230 us
    reduce_scatter x4, waiting for transfers between devices, micro_step(): lax.psum_scatter(contract_cols(mixed_group, project_full).astype(jnp.bflo...  87 us
    reduce_scatter x4, waiting for transfers between devices, micro_step(): lax.psum_scatter(jnp.dot(hidden, reduce_full, preferred_element_type=jnp....  63.6 us
    psum x1, waiting for transfers between devices, micro_step(): lax.psum((slot_four * key_value_state[None], slot_three * norm_total[None...  59.8 us
    reduce_scatter x4, waiting for transfers between devices, micro_step(): lax.psum_scatter(contract_cols(pre_grad, expand_full).astype(jnp.bfloat16...  41.3 us
    psum x1, blocking collectives, micro_step(): lax.psum((slot_four * key_value_state[None], slot_three * norm_total[None...  39.9 us
  transfers between devices with their start and end apart: 47, of which 32 were waited for; matrix products, arithmetic and copies ran while one was open for 11% of the time, Pallas kernels for 0%

commit v1 on v0

--- a/solution.py
+++ b/solution.py
@@ -156,9 +156,8 @@
         seq_bound = lengths[micro_index * seq_slots + seq_place]
         keep_mask = (positions < seq_bound).astype(jnp.float32)
         key_value_state, norm_total = key_summary(key_rows, value_matrix, keep_mask, projection)
-        state_sums = lax.psum(
-            (slot_four * key_value_state[None], slot_three * norm_total[None]), ("row", "col")
-        )
+        half = lax.psum((slot_four * key_value_state[None], slot_three * norm_total[None]), "col")
+        state_sums = lax.psum(half, "row")
         state_all = jnp.sum(slot_four * state_sums[0], axis=0)
         total_all = jnp.sum(slot_three * state_sums[1], axis=0)
         attended = (

time: 1900 us -> 2270 us (1.19)
  waiting for transfers between devices: 1380 us -> 1740 us
    reduce_scatter x4, waiting for transfers between devices: 28.9 us -> 255 us  [reduce_grads(): lax.psum_scatter(expand_sum.astype(jnp.bfloat16), 'row', scatter_dimensio...]
    reduce_scatter x4, waiting for transfers between devices: 0.08 us -> 47.9 us  [reduce_grads(): lax.psum_scatter(combine_sum.astype(jnp.bfloat16), 'col', scatter_dimensi...]
    psum x0 -> x1, blocking collectives: none -> 37.9 us  [micro_step(): state_sums = lax.psum(half, 'row')]
    all_gather x1, waiting for transfers between devices: 0.01 us -> 37.5 us  [fetch_weights(): lax.all_gather(reduce_cols, 'row', axis=1, tiled=True)]
    psum x0 -> x1, waiting for transfers between devices: none -> 37.2 us  [micro_step(): state_sums = lax.psum(half, 'row')]
    psum x1, blocking collectives: 39.9 us -> 11.6 us  [micro_step(): lax.psum((slot_four * key_value_state[None], slot_three * norm_total[None...]
    all_gather x1, waiting for transfers between devices: 0.01 us -> 22.9 us  [fetch_weights(): lax.all_gather(expand_cols, 'row', axis=0, tiled=True)]
    unnamed x48 -> x49, waiting for transfers between devices: 585 us -> 584 us
  transfers between devices with their start and end apart: 47 -> 48, of which waited for: 32 -> 41; matrix products, arithmetic and copies ran while one was open for 11% -> 9% of each run, Pallas kernels for 0% -> 0%
where the time goes in v1:
time: 2270 us
  waiting for transfers between devices  1740 us (77%)
  blocking collectives  203 us (9%)
  matrix products  131 us (6%)
  local copies, waits for them, and re-layouts  79.8 us (4%)
  other arithmetic  58.9 us (3%)
  starting transfers between devices  31 us (1%)
    unnamed x49, waiting for transfers between devices  584 us
    reduce_scatter x4, waiting for transfers between devices, reduce_grads(): lax.psum_scatter(reduce_sum.astype(jnp.bfloat16), 'row', scatter_dimensio...  262 us
    reduce_scatter x4, waiting for transfers between devices, reduce_grads(): lax.psum_scatter(expand_sum.astype(jnp.bfloat16), 'row', scatter_dimensio...  255 us
    psum x2, waiting for transfers between devices, micro_step(): lax.psum((slot_four * state_grad[None], slot_three * total_grad[None], sm...  213 us
    reduce_scatter x4, waiting for transfers between devices, micro_step(): lax.psum_scatter(contract_cols(mixed_group, project_full).astype(jnp.bflo...  87.4 us
    psum x1, waiting for transfers between devices, micro_step(): lax.psum((slot_four * key_value_state[None], slot_three * norm_total[None...  69.1 us
    reduce_scatter x4, waiting for transfers between devices, reduce_grads(): lax.psum_scatter(combine_sum.astype(jnp.bfloat16), 'col', scatter_dimensi...  47.9 us
    reduce_scatter x4, waiting for transfers between devices, micro_step(): lax.psum_scatter(jnp.dot(hidden, reduce_full, preferred_element_type=jnp....  47.6 us
  transfers between devices with their start and end apart: 48, of which 41 were waited for; matrix products, arithmetic and copies ran while one was open for 9% of the time, Pallas kernels for 0%

profile of v1, /device:TPU:0, one launch (start us, length us, event | category | flops | bytes accessed | tf_op | source)
XLA Modules:
  0.0 2268.2 jit_solution(4876752479193503365)
XLA Ops:
  7.2 34.7 %all_gather.67 = bf16[768,576]{1,0:T(8,128)(2,1)S(1)} all-gather(bf16[96,576]{1,0:T(8,128)(2,1)} %param.18), channel_id=1, replica_groups=mesh['row'=8,'col'=4] {'row'}, dimensions={0}, use_global_device_ids=true | all-gather | bytes 995328 | tf_op jit(solution)/shard_map/all_gather | solution.py:60
  42.0 6.5 all-gather
  54.1 9.7 all-gather.2
  66.0 6.6 all-gather.1
  72.5 3.5 all-to-all-start.2
  77.5 8.2 all-gather.3
  91.2 4.6 all-to-all-done.1
  95.8 3.5 all-to-all-start.3
  122.1 69.1 %all-reduce.27.cloned.1.call-done = (f32[1,12,256,64]{2,3,1,0:T(8,128)}, f32[1,12,256,64]{2,3,1,0:T(8,128)}, f32[1,12,256,64]{2,3,1,0:T(8,128)}, f32[1,12,256,64]{2,3,1,0:T(8,128)}) async-done(((f32[1,12,256,64]{2,3,1,0:T(8,128)}, f32[1,12,256,64]{2,3,1,0:T(8,128)}, f32[1,12,256,64]{2,3,1,0:T(8,128)}, f32[1,12,256,64]{2,3,1,0:T(8,128)}), (f32[1,12,256,64]{2,3,1,0:T(8,128)}, f32[1,12,256,64]{2,3,1,0:T(8,128)}, ...) | async-done | bytes 3145744 | tf_op jit(solution)/shard_map/psum | solution.py:159
  192.0 32.6 %all_gather.68 = bf16[768,192]{1,0:T(8,128)(2,1)S(1)} all-gather(bf16[96,192]{1,0:T(8,128)(2,1)S(1)} %copy-done.168), channel_id=1, replica_groups=mesh['row'=8,'col'=4] {'row'}, dimensions={0}, use_global_device_ids=true | all-gather | bytes 331776 | tf_op jit(solution)/shard_map/all_gather | solution.py:61
  230.4 11.6 all-reduce.12
  242.0 37.9 %all-reduce.10 = (f32[1,12,256]{2,1,0:T(8,128)S(1)}, f32[1,12,256]{2,1,0:T(8,128)S(1)}, f32[1,12,256]{2,1,0:T(8,128)S(1)}, f32[1,12,256]{2,1,0:T(8,128)S(1)}) all-reduce(f32[1,12,256]{2,1,0:T(8,128)S(1)} %get-tuple-element.141, f32[1,12,256]{2,1,0:T(8,128)S(1)} %get-tuple-element.142, ...), channel_id=1, replica_groups=mesh['row'=8,'col'=4] {'row'}, use_global_device_ids=true, to_apply=%region_6.7 | all-reduce | flops 12288 | bytes 98304 | tf_op jit(solution)/shard_map/psum | solution.py:160
  291.4 37.2 %all-reduce.25.cloned.1.call-done = (f32[1,12,256,64]{2,3,1,0:T(8,128)}, f32[1,12,256,64]{2,3,1,0:T(8,128)}, f32[1,12,256,64]{2,3,1,0:T(8,128)}, f32[1,12,256,64]{2,3,1,0:T(8,128)}) async-done(((f32[1,12,256,64]{2,3,1,0:T(8,128)}, f32[1,12,256,64]{2,3,1,0:T(8,128)}, f32[1,12,256,64]{2,3,1,0:T(8,128)}, f32[1,12,256,64]{2,3,1,0:T(8,128)}), (f32[1,12,256,64]{2,3,1,0:T(8,128)}, f32[1,12,256,64]{2,3,1,0:T(8,128)}, ...) | async-done | bytes 3145744 | tf_op jit(solution)/shard_map/psum | solution.py:160
  331.4 15.9 all-gather.8.cloned.1.call-done
  360.6 7.1 all_gather.70
  367.7 22.9 %all-gather.10.cloned.1.call-done = bf16[768,768]{1,0:T(8,128)(2,1)} async-done(((bf16[96,768]{1,0:T(8,128)(2,1)}), bf16[768,768]{1,0:T(8,128)(2,1)}) %all-gather.10.cloned.1.call-update) | async-done | bytes 1179664 | tf_op jit(solution)/shard_map/all_gather | solution.py:62
  390.6 4.6 multiply_convert_fusion.3
  395.3 37.5 %all-gather.12.cloned.1.call-done = bf16[768,768]{0,1:T(8,128)(2,1)} async-done(((bf16[768,96]{0,1:T(8,128)(2,1)}), bf16[768,768]{0,1:T(8,128)(2,1)}) %all-gather.12.cloned.1.call-update) | async-done | bytes 1179664 | tf_op jit(solution)/shard_map/all_gather | solution.py:63
  435.5 6.6 all_gather.76
  442.1 7.0 all_gather.74
  449.1 8.6 all_gather.78
  462.9 4.6 multiply_convert_fusion.2
  469.7 4.7 multiply_convert_fusion
  478.0 4.9 reduce-scatter.53.cloned.1.call-done
  487.2 19.1 reduce-scatter.51.cloned.1.call-done
  506.4 23.5 %reduce-scatter.55.cloned.1.call-done = bf16[64,768]{1,0:T(8,128)(2,1)} async-done(((bf16[256,768]{1,0:T(8,128)(2,1)}), bf16[64,768]{1,0:T(8,128)(2,1)}) %reduce-scatter.55.cloned.1.call-update) | async-done | bytes 98320 | tf_op jit(solution)/shard_map/reduce_scatter | solution.py:175
  537.5 6.1 all_gather.81
  548.2 7.0 all_gather.80
  555.3 6.6 all_gather.82
  577.0 6.6 all_gather.79
  593.9 21.2 reduce-scatter.61.cloned.1.call-done
  620.7 18.0 reduce-scatter.57.cloned.1.call-done
  709.5 69.6 %all-reduce.21.cloned.1.call-done = (f32[1,12,256]{2,1,0:T(8,128)}, f32[1,12,256]{2,1,0:T(8,128)}, f32[1,12,256]{2,1,0:T(8,128)}, f32[1,12,256]{2,1,0:T(8,128)}, f32[6,768]{1,0:T(8,128)}) async-done(((f32[1,12,256]{2,1,0:T(8,128)}, f32[1,12,256]{2,1,0:T(8,128)}, f32[1,12,256]{2,1,0:T(8,128)}, f32[1,12,256]{2,1,0:T(8,128)}, f32[6,768]{1,0:T(8,128)}), (f32[1,12,256]{2,1,0:T(8,128)}, f32[1,12,256]{2,1,0:T(8,128)}, ...) | async-done | bytes 67600 | tf_op jit(solution)/shard_map/psum | solution.py:228
  781.9 143.8 %all-reduce.23.cloned.1.call-done = (f32[1,12,256,64]{2,3,1,0:T(8,128)}, f32[1,12,256,64]{2,3,1,0:T(8,128)}, f32[1,12,256,64]{2,3,1,0:T(8,128)}, f32[1,12,256,64]{2,3,1,0:T(8,128)}) async-done(((f32[1,12,256,64]{2,3,1,0:T(8,128)}, f32[1,12,256,64]{2,3,1,0:T(8,128)}, f32[1,12,256,64]{2,3,1,0:T(8,128)}, f32[1,12,256,64]{2,3,1,0:T(8,128)}), (f32[1,12,256,64]{2,3,1,0:T(8,128)}, f32[1,12,256,64]{2,3,1,0:T(8,128)}, ...) | async-done | bytes 3145744 | tf_op jit(solution)/shard_map/psum | solution.py:228
  931.5 3.5 all-to-all-start.7
  946.5 3.5 all-to-all-start.6
  951.1 5.6 all-to-all-done.6
  956.7 3.7 all-to-all-start.5
  961.6 5.4 all-to-all-done.5
  967.0 3.5 all-to-all-start.4
  975.4 4.6 all-to-all-done.4
  990.3 21.3 reduce-scatter.75.cloned.1.call-done
  1013.6 26.6 %reduce-scatter.73.cloned.1.call-done = bf16[768,192]{0,1:T(8,128)(2,1)} async-done(((bf16[768,768]{0,1:T(8,128)(2,1)}), bf16[768,192]{0,1:T(8,128)(2,1)}) %reduce-scatter.73.cloned.1.call-update) | async-done | bytes 294928 | tf_op jit(solution)/shard_map/reduce_scatter | solution.py:77
  1051.1 56.3 %reduce-scatter.87.cloned.1.call-done = bf16[96,768]{1,0:T(8,128)(2,1)} async-done(((bf16[768,768]{1,0:T(8,128)(2,1)}), bf16[96,768]{1,0:T(8,128)(2,1)}) %reduce-scatter.87.cloned.1.call-update) | async-done | bytes 147472 | tf_op jit(solution)/shard_map/reduce_scatter | solution.py:86
  1107.3 66.4 %reduce-scatter.85.cloned.1.call-done = bf16[96,768]{1,0:T(8,128)(2,1)} async-done(((bf16[768,768]{1,0:T(8,128)(2,1)}), bf16[96,768]{1,0:T(8,128)(2,1)}) %reduce-scatter.85.cloned.1.call-update) | async-done | bytes 147472 | tf_op jit(solution)/shard_map/reduce_scatter | solution.py:86
  1173.8 66.4 %reduce-scatter.83.cloned.1.call-done = bf16[96,768]{1,0:T(8,128)(2,1)} async-done(((bf16[768,768]{1,0:T(8,128)(2,1)}), bf16[96,768]{1,0:T(8,128)(2,1)}) %reduce-scatter.83.cloned.1.call-update) | async-done | bytes 147472 | tf_op jit(solution)/shard_map/reduce_scatter | solution.py:86
  1240.2 66.4 %reduce-scatter.81.cloned.1.call-done = bf16[96,768]{1,0:T(8,128)(2,1)} async-done(((bf16[768,768]{1,0:T(8,128)(2,1)}), bf16[96,768]{1,0:T(8,128)(2,1)}) %reduce-scatter.81.cloned.1.call-update) | async-done | bytes 147472 | tf_op jit(solution)/shard_map/reduce_scatter | solution.py:86
  1310.3 62.7 %reduce-scatter.95.cloned.1.call-done = bf16[768,96]{0,1:T(8,128)(2,1)} async-done(((bf16[768,768]{0,1:T(8,128)(2,1)}), bf16[768,96]{0,1:T(8,128)(2,1)}) %reduce-scatter.95.cloned.1.call-update) | async-done | bytes 147472 | tf_op jit(solution)/shard_map/reduce_scatter | solution.py:89
  1373.0 66.6 %reduce-scatter.93.cloned.1.call-done = bf16[768,96]{0,1:T(8,128)(2,1)} async-done(((bf16[768,768]{0,1:T(8,128)(2,1)}), bf16[768,96]{0,1:T(8,128)(2,1)}) %reduce-scatter.93.cloned.1.call-update) | async-done | bytes 147472 | tf_op jit(solution)/shard_map/reduce_scatter | solution.py:89
  1439.6 66.3 %reduce-scatter.91.cloned.1.call-done = bf16[768,96]{0,1:T(8,128)(2,1)} async-done(((bf16[768,768]{0,1:T(8,128)(2,1)}), bf16[768,96]{0,1:T(8,128)(2,1)}) %reduce-scatter.91.cloned.1.call-update) | async-done | bytes 147472 | tf_op jit(solution)/shard_map/reduce_scatter | solution.py:89
  1505.9 66.3 %reduce-scatter.89.cloned.1.call-done = bf16[768,96]{0,1:T(8,128)(2,1)} async-done(((bf16[768,768]{0,1:T(8,128)(2,1)}), bf16[768,96]{0,1:T(8,128)(2,1)}) %reduce-scatter.89.cloned.1.call-update) | async-done | bytes 147472 | tf_op jit(solution)/shard_map/reduce_scatter | solution.py:89
  1574.1 73.2 %all-reduce.29.cloned.1.call-done = (bf16[4608]{0:T(1024)(128)(2,1)}, bf16[4608]{0:T(1024)(128)(2,1)}, bf16[4608]{0:T(1024)(128)(2,1)}, bf16[4608]{0:T(1024)(128...) async-done(((bf16[4608]{0:T(1024)(128)(2,1)}, bf16[4608]{0:T(1024)(128)(2,1)}, ...) | async-done | bytes 86032
  1650.0 20.5 reduce-scatter.71.cloned.1.call-done
  1671.4 22.2 reduce-scatter.67.cloned.1.call-done
  1694.6 22.4 reduce-scatter.63.cloned.1.call-done
  1717.9 22.4 reduce-scatter.59.cloned.1.call-done
  1742.2 62.6 %reduce-scatter.111.cloned.1.call-done = bf16[96,192]{1,0:T(8,128)(2,1)} async-done(((bf16[768,192]{1,0:T(8,128)(2,1)}), bf16[96,192]{1,0:T(8,128)(2,1)}) %reduce-scatter.111.cloned.1.call-update) | async-done | bytes 36880
  1805.7 62.8 %reduce-scatter.109.cloned.1.call-done = bf16[96,192]{1,0:T(8,128)(2,1)} async-done(((bf16[768,192]{1,0:T(8,128)(2,1)}), bf16[96,192]{1,0:T(8,128)(2,1)}) %reduce-scatter.109.cloned.1.call-update) | async-done | bytes 36880
  1869.4 62.7 %reduce-scatter.107.cloned.1.call-done = bf16[96,192]{1,0:T(8,128)(2,1)} async-done(((bf16[768,192]{1,0:T(8,128)(2,1)}), bf16[96,192]{1,0:T(8,128)(2,1)}) %reduce-scatter.107.cloned.1.call-update) | async-done | bytes 36880
  1933.1 62.7 %reduce-scatter.105.cloned.1.call-done = bf16[96,192]{1,0:T(8,128)(2,1)} async-done(((bf16[768,192]{1,0:T(8,128)(2,1)}), bf16[96,192]{1,0:T(8,128)(2,1)}) %reduce-scatter.105.cloned.1.call-update) | async-done | bytes 36880
  1997.4 63.9 %reduce-scatter.103.cloned.1.call-done = bf16[96,576]{1,0:T(8,128)(2,1)} async-done(((bf16[768,576]{1,0:T(8,128)(2,1)}), bf16[96,576]{1,0:T(8,128)(2,1)}) %reduce-scatter.103.cloned.1.call-update) | async-done | bytes 110608
  2062.4 65.0 %reduce-scatter.101.cloned.1.call-done = bf16[96,576]{1,0:T(8,128)(2,1)} async-done(((bf16[768,576]{1,0:T(8,128)(2,1)}), bf16[96,576]{1,0:T(8,128)(2,1)}) %reduce-scatter.101.cloned.1.call-update) | async-done | bytes 110608
  2128.5 64.6 %reduce-scatter.99.cloned.1.call-done = bf16[96,576]{1,0:T(8,128)(2,1)} async-done(((bf16[768,576]{1,0:T(8,128)(2,1)}), bf16[96,576]{1,0:T(8,128)(2,1)}) %reduce-scatter.99.cloned.1.call-update) | async-done | bytes 110608
  2194.1 65.1 %reduce-scatter.97.cloned.1.call-done = bf16[96,576]{1,0:T(8,128)(2,1)} async-done(((bf16[768,576]{1,0:T(8,128)(2,1)}), bf16[96,576]{1,0:T(8,128)(2,1)}) %reduce-scatter.97.cloned.1.call-update) | async-done | bytes 110608
  (1018 shorter events, 271.7 us)
Async XLA Ops:
  7.2 105.3 %copy-start = (f32[256,64]{0,1:T(8,128)S(1)}, f32[256,64]{0,1:T(8,128)}, u32[]{:S(2)}) copy-start(f32[256,64]{0,1:T(8,128)} %param.30) | copy-start | bytes 196612
  50.6 21.9 all-to-all-start
  72.5 13.1 all-to-all-start.2
  85.7 10.2 all-to-all-start.1
  95.8 10.2 all-to-all-start.3
  99.3 91.9 %all-reduce.27.cloned.1.call-start = ((), (), s32[]{:S(2)}) async-start(), calls=%async_computation.78 | async-start | bytes 6291456 | tf_op jit(solution)/shard_map/psum | solution.py:159
  122.0 206.6 %all-reduce.25.cloned.1.call-start = ((), (), s32[]{:S(2)}) async-start(), calls=%async_computation.77 | async-start | bytes 6291456 | tf_op jit(solution)/shard_map/psum | solution.py:160
  191.2 156.0 %all-gather.8.cloned.1.call-start = ((), (), s32[]{:S(2)}) async-start(), calls=%async_computation.40 | async-start | bytes 1474560 | tf_op jit(solution)/shard_map/all_gather | solution.py:65
  225.4 165.2 %all-gather.10.cloned.1.call-start = ((), (), s32[]{:S(2)}) async-start(), calls=%async_computation.41 | async-start | bytes 1327104 | tf_op jit(solution)/shard_map/all_gather | solution.py:62
  226.0 206.7 %all-gather.12.cloned.1.call-start = ((), (), s32[]{:S(2)}) async-start(), calls=%async_computation.42 | async-start | bytes 1327104 | tf_op jit(solution)/shard_map/all_gather | solution.py:63
  226.6 250.3 %reduce-scatter.49.cloned.1.call-start = ((), (), s32[]{:S(2)}) async-start(), calls=%async_computation.43 | async-start | bytes 491520 | tf_op jit(solution)/shard_map/reduce_scatter | solution.py:175
  354.7 237.0 %copy-start.38 = (f32[64,768]{1,0:T(8,128)}, f32[64,768]{1,0:T(8,128)S(1)}, u32[]{:S(2)}) copy-start(f32[64,768]{1,0:T(8,128)S(1)} %get-tuple-element.285) | copy-start | bytes 589828
  435.5 47.4 %reduce-scatter.53.cloned.1.call-start = ((), (), s32[]{:S(2)}) async-start(), calls=%async_computation.45 | async-start | bytes 491520 | tf_op jit(solution)/shard_map/reduce_scatter | solution.py:175
  462.9 43.5 %reduce-scatter.51.cloned.1.call-start = ((), (), s32[]{:S(2)}) async-start(), calls=%async_computation.44 | async-start | bytes 491520 | tf_op jit(solution)/shard_map/reduce_scatter | solution.py:175
  469.6 60.3 %reduce-scatter.55.cloned.1.call-start = ((), (), s32[]{:S(2)}) async-start(), calls=%async_computation.46 | async-start | bytes 491520 | tf_op jit(solution)/shard_map/reduce_scatter | solution.py:175
  476.4 112.7 %reduce-scatter.65.cloned.1.call-start = ((), (), s32[]{:S(2)}) async-start(), calls=%async_computation.51 | async-start | bytes 491520 | tf_op jit(solution)/shard_map/reduce_scatter | solution.py:196
  536.3 78.9 %copy-start.225 = (f32[64]{0:T(128)}, f32[64]{0:T(128)S(1)}, u32[]{:S(2)}) copy-start(f32[64]{0:T(128)S(1)} %negate_multiply_fusion.17) | copy-start | bytes 772
  547.0 44.8 %reduce-scatter.69.cloned.1.call-start = ((), (), s32[]{:S(2)}) async-start(), calls=%async_computation.53 | async-start | bytes 491520 | tf_op jit(solution)/shard_map/reduce_scatter | solution.py:196
  566.8 48.4 %reduce-scatter.61.cloned.1.call-start = ((), (), s32[]{:S(2)}) async-start(), calls=%async_computation.49 | async-start | bytes 491520 | tf_op jit(solution)/shard_map/reduce_scatter | solution.py:196
  572.1 66.5 %reduce-scatter.57.cloned.1.call-start = ((), (), s32[]{:S(2)}) async-start(), calls=%async_computation.47 | async-start | bytes 491520 | tf_op jit(solution)/shard_map/reduce_scatter | solution.py:196
  588.8 190.3 %all-reduce.21.cloned.1.call-start = ((), (), s32[]{:S(2)}) async-start(), calls=%async_computation.75 | async-start | bytes 180224 | tf_op jit(solution)/shard_map/psum | solution.py:228
  656.5 269.2 %all-reduce.23.cloned.1.call-start = ((), (), s32[]{:S(2)}) async-start(), calls=%async_computation.76 | async-start | bytes 6291456 | tf_op jit(solution)/shard_map/psum | solution.py:228
  658.4 327.9 %reduce-scatter.79.cloned.1.call-start = ((), (), s32[]{:S(2)}) async-start(), calls=%async_computation.58 | async-start | bytes 1474560 | tf_op jit(solution)/shard_map/reduce_scatter | solution.py:77
  660.9 327.5 %reduce-scatter.77.cloned.1.call-start = ((), (), s32[]{:S(2)}) async-start(), calls=%async_computation.57 | async-start | bytes 1474560 | tf_op jit(solution)/shard_map/reduce_scatter | solution.py:77
  662.5 349.1 %reduce-scatter.75.cloned.1.call-start = ((), (), s32[]{:S(2)}) async-start(), calls=%async_computation.56 | async-start | bytes 1474560 | tf_op jit(solution)/shard_map/reduce_scatter | solution.py:77
  664.2 376.0 %reduce-scatter.73.cloned.1.call-start = ((), (), s32[]{:S(2)}) async-start(), calls=%async_computation.55 | async-start | bytes 1474560 | tf_op jit(solution)/shard_map/reduce_scatter | solution.py:77
  665.8 441.5 %reduce-scatter.87.cloned.1.call-start = ((), (), s32[]{:S(2)}) async-start(), calls=%async_computation.62 | async-start | bytes 1327104 | tf_op jit(solution)/shard_map/reduce_scatter | solution.py:86
  668.9 504.9 %reduce-scatter.85.cloned.1.call-start = ((), (), s32[]{:S(2)}) async-start(), calls=%async_computation.61 | async-start | bytes 1327104 | tf_op jit(solution)/shard_map/reduce_scatter | solution.py:86
  671.5 568.6 %reduce-scatter.83.cloned.1.call-start = ((), (), s32[]{:S(2)}) async-start(), calls=%async_computation.60 | async-start | bytes 1327104 | tf_op jit(solution)/shard_map/reduce_scatter | solution.py:86
  674.2 632.3 %reduce-scatter.81.cloned.1.call-start = ((), (), s32[]{:S(2)}) async-start(), calls=%async_computation.59 | async-start | bytes 1327104 | tf_op jit(solution)/shard_map/reduce_scatter | solution.py:86
  676.9 696.0 %reduce-scatter.95.cloned.1.call-start = ((), (), s32[]{:S(2)}) async-start(), calls=%async_computation.66 | async-start | bytes 1327104 | tf_op jit(solution)/shard_map/reduce_scatter | solution.py:89
  679.6 759.9 %reduce-scatter.93.cloned.1.call-start = ((), (), s32[]{:S(2)}) async-start(), calls=%async_computation.65 | async-start | bytes 1327104 | tf_op jit(solution)/shard_map/reduce_scatter | solution.py:89
  682.3 823.5 %reduce-scatter.91.cloned.1.call-start = ((), (), s32[]{:S(2)}) async-start(), calls=%async_computation.64 | async-start | bytes 1327104 | tf_op jit(solution)/shard_map/reduce_scatter | solution.py:89
  684.9 887.2 %reduce-scatter.89.cloned.1.call-start = ((), (), s32[]{:S(2)}) async-start(), calls=%async_computation.63 | async-start | bytes 1327104 | tf_op jit(solution)/shard_map/reduce_scatter | solution.py:89
  707.7 218.1 %copy-start.29 = (f32[64,12,256]{2,0,1:T(8,128)S(1)}, f32[64,12,256]{2,0,1:T(8,128)}, u32[]{:S(2)}) copy-start(f32[64,12,256]{2,0,1:T(8,128)} %copy-done.28) | copy-start | bytes 2359300
  707.7 218.1 %copy-start.214 = (f32[64]{0:T(128)S(1)}, f32[64]{0:T(128)}, u32[]{:S(2)}) copy-start(f32[64]{0:T(128)} %copy-done.213) | copy-start | bytes 772
  709.5 218.6 %copy-start.70 = (bf16[64,768]{0,1:T(8,128)(2,1)S(1)}, bf16[64,768]{0,1:T(8,128)(2,1)}, u32[]{:S(2)}) copy-start(bf16[64,768]{0,1:T(8,128)(2,1)} %copy-done.69) | copy-start | bytes 294916
  709.5 218.6 %copy-start.246 = (f32[64]{0:T(128)S(1)}, f32[64]{0:T(128)}, u32[]{:S(2)}) copy-start(f32[64]{0:T(128)} %get-tuple-element.310) | copy-start | bytes 772
  931.5 15.0 all-to-all-start.7
  946.5 10.2 all-to-all-start.6
  956.7 10.4 all-to-all-start.5
  967.0 13.0 all-to-all-start.4
  970.5 676.7 %all-reduce.29.cloned.1.call-start = ((), (), s32[]{:S(2)}) async-start(), calls=%async_computation.79 | async-start | bytes 180224
  980.8 689.6 %reduce-scatter.71.cloned.1.call-start = ((), (), s32[]{:S(2)}) async-start(), calls=%async_computation.54 | async-start | bytes 491520 | tf_op jit(solution)/shard_map/reduce_scatter | solution.py:251
  982.2 711.4 %reduce-scatter.67.cloned.1.call-start = ((), (), s32[]{:S(2)}) async-start(), calls=%async_computation.52 | async-start | bytes 491520 | tf_op jit(solution)/shard_map/reduce_scatter | solution.py:251
  983.5 733.4 %reduce-scatter.63.cloned.1.call-start = ((), (), s32[]{:S(2)}) async-start(), calls=%async_computation.50 | async-start | bytes 491520 | tf_op jit(solution)/shard_map/reduce_scatter | solution.py:251
  984.9 755.4 %reduce-scatter.59.cloned.1.call-start = ((), (), s32[]{:S(2)}) async-start(), calls=%async_computation.48 | async-start | bytes 491520 | tf_op jit(solution)/shard_map/reduce_scatter | solution.py:251
  986.2 818.6 %reduce-scatter.111.cloned.1.call-start = ((), (), s32[]{:S(2)}) async-start(), calls=%async_computation.74 | async-start | bytes 442368
  988.3 880.3 %reduce-scatter.109.cloned.1.call-start = ((), (), s32[]{:S(2)}) async-start(), calls=%async_computation.73 | async-start | bytes 442368
  990.3 941.9 %reduce-scatter.107.cloned.1.call-start = ((), (), s32[]{:S(2)}) async-start(), calls=%async_computation.72 | async-start | bytes 442368
  1013.5 982.3 %reduce-scatter.105.cloned.1.call-start = ((), (), s32[]{:S(2)}) async-start(), calls=%async_computation.71 | async-start | bytes 442368
  1042.0 1019.4 %reduce-scatter.103.cloned.1.call-start = ((), (), s32[]{:S(2)}) async-start(), calls=%async_computation.70 | async-start | bytes 1105920
  1043.9 1083.6 %reduce-scatter.101.cloned.1.call-start = ((), (), s32[]{:S(2)}) async-start(), calls=%async_computation.69 | async-start | bytes 1105920
  1045.7 1147.3 %reduce-scatter.99.cloned.1.call-start = ((), (), s32[]{:S(2)}) async-start(), calls=%async_computation.68 | async-start | bytes 1105920
  1047.6 260.8 %copy-start.106 = (bf16[1,256,768]{2,1,0:T(8,128)(2,1)S(1)}, bf16[1,256,768]{2,1,0:T(8,128)(2,1)}, u32[]{:S(2)}) copy-start(bf16[1,256,768]{2,1,0:T(8,128)(2,1)} %copy-done.105) | copy-start | bytes 1179652
  1047.6 1211.5 %reduce-scatter.97.cloned.1.call-start = ((), (), s32[]{:S(2)}) async-start(), calls=%async_computation.67 | async-start | bytes 1105920
  1310.2 360.2 %copy-start.84 = (f32[64,768]{1,0:T(8,128)S(1)}, f32[64,768]{1,0:T(8,128)}, u32[]{:S(2)}) copy-start(f32[64,768]{1,0:T(8,128)} %copy-done.83) | copy-start | bytes 589828
  1310.2 360.2 %copy-start.236 = (f32[64]{0:T(128)S(1)}, f32[64]{0:T(128)}, u32[]{:S(2)}) copy-start(f32[64]{0:T(128)} %copy-done.235) | copy-start | bytes 772
  1310.2 383.4 %copy-start.86 = (f32[64,768]{1,0:T(8,128)S(1)}, f32[64,768]{1,0:T(8,128)}, u32[]{:S(2)}) copy-start(f32[64,768]{1,0:T(8,128)} %copy-done.85) | copy-start | bytes 589828
  1310.2 383.4 %copy-start.238 = (f32[64]{0:T(128)S(1)}, f32[64]{0:T(128)}, u32[]{:S(2)}) copy-start(f32[64]{0:T(128)} %copy-done.237) | copy-start | bytes 772
  1310.3 406.7 %copy-start.74 = (f32[64,768]{1,0:T(8,128)S(1)}, f32[64,768]{1,0:T(8,128)}, u32[]{:S(2)}) copy-start(f32[64,768]{1,0:T(8,128)} %copy-done.73) | copy-start | bytes 589828
  1310.3 406.7 %copy-start.242 = (f32[64]{0:T(128)S(1)}, f32[64]{0:T(128)}, u32[]{:S(2)}) copy-start(f32[64]{0:T(128)} %copy-done.241) | copy-start | bytes 772
  1310.3 430.0 %copy-start.72 = (f32[64,768]{1,0:T(8,128)S(1)}, f32[64,768]{1,0:T(8,128)}, u32[]{:S(2)}) copy-start(f32[64,768]{1,0:T(8,128)} %copy-done.71) | copy-start | bytes 589828
  1310.3 430.0 %copy-start.240 = (f32[64]{0:T(128)S(1)}, f32[64]{0:T(128)}, u32[]{:S(2)}) copy-start(f32[64]{0:T(128)} %copy-done.239) | copy-start | bytes 772
  (259 other events, 1433.3 us)
Sparse Core Ops, SparseCore 0:
  122.1 68.9 all-reduce.26
  195.1 133.4 all-reduce.24
  330.8 16.4 all-gather.7
  349.5 41.0 all-gather.9
  392.9 39.8 all-gather.11
  435.6 21.5 reduce-scatter.48
  463.0 19.8 reduce-scatter.52
  485.5 20.8 reduce-scatter.50
  509.0 20.8 reduce-scatter.54
  547.1 21.1 reduce-scatter.64
  570.9 20.8 reduce-scatter.68
  594.3 20.8 reduce-scatter.60
  617.8 20.8 reduce-scatter.56
  656.6 122.3 all-reduce.20
  785.9 139.8 all-reduce.22
  928.2 24.8 reduce-scatter.78
  955.7 28.7 reduce-scatter.76
  986.9 24.6 reduce-scatter.74
  1014.3 25.7 reduce-scatter.72
  1043.4 63.9 reduce-scatter.86
  1110.7 63.0 reduce-scatter.84
  1177.2 62.9 reduce-scatter.82
  1243.6 62.9 reduce-scatter.80
  1309.8 63.1 reduce-scatter.94
  1376.4 63.1 reduce-scatter.92
  1442.8 63.0 reduce-scatter.90
  1509.1 63.0 reduce-scatter.88
  1577.0 70.1 all-reduce.28
  1650.3 20.0 reduce-scatter.70
  1672.8 20.7 reduce-scatter.66
  1696.1 20.7 reduce-scatter.62
  1719.5 20.7 reduce-scatter.58
  1743.4 61.3 reduce-scatter.110
  1808.1 60.3 reduce-scatter.108
  1871.8 60.3 reduce-scatter.106
  1935.3 60.4 reduce-scatter.104
  1998.9 62.3 reduce-scatter.102
  2065.1 62.3 reduce-scatter.100
  2130.6 62.3 reduce-scatter.98
  2196.7 62.3 reduce-scatter.96
